TPU v7x, 512 devices: a whole 4x8x8 slice. The times are simulated.
512 devices in a mesh: owner: 128 (over y, z, core), rep: 4 (over x).
Axes of the slice: x: 4, y: 8, z: 8, core: 2. Of those that a mesh axis runs over, the one named last changes fastest.
Arguments:
- bin_blocks: int32 [131072], P(('owner', 'rep')), may hold values from 0 to 32767, as said below
- send_counts: int32 [512, 128], P(('owner', 'rep')), may hold values from 0 to 4, as said below
- voxel_index: int32 [131072, 128], P(('owner', 'rep')), may hold values from 0 to 511
- point_sdf: bfloat16 [131072, 128], P(('owner', 'rep')), may hold values from -1 to 1
- point_weight: bfloat16 [131072, 128], P(('owner', 'rep')), may hold values from 0.099609375 to 1
- point_color: bfloat16 [131072, 3, 128], P(('owner', 'rep')), may hold values from 0 to 1
- owner_table: int32 [32768], replicated, may hold values from 0 to 32767, as said below
- old_tsdf: float32 [32768, 4, 512], P(('owner', 'rep')), may hold values from -1 to 1
- old_weight: float32 [32768, 512], P(('owner', 'rep')), may hold values from 0.5 to 4
Outputs:
- new_tsdf: float32 [32768, 4, 512], P(('owner', 'rep'))
- new_weight: float32 [32768, 512], P(('owner', 'rep'))
Inputs may be any that keep to these rules, and one draw needn't show every extreme that they name: `send_counts`: each row sums to 256; every row has an entry equal to 4; among the devices s with the same s mod 4 (one frame group), some owner receives 4 bins from every one of them. `owner_table`: a permutation; entry g is the owner of block g times 256 plus the block's place among that owner's blocks. `bin_blocks`: owner_table assigns the block of bin j of device s to owner p(s, j) of the first step; of the bins that one frame group sends to one owner, at most 128 have places in any one quarter of its 256 places (places q * 64 to (q + 1) * 64 - 1), and this most is reached in every frame group.
All inputs are finite; a program needn't handle non-finite values.
Results may differ from a plain program's by a relative error of at most 0.00078.
Values may be sent and summed in bfloat16 or wider, within the bound.
No kernel may reach another device: no remote copies, remote signals or barrier semaphores. Data moves between devices by JAX's collectives and lax.ppermute only.
A program may use at most 64 MiB of HBM per device.

v0:
```python
import math
import jax
import jax.numpy as jnp
from jax import lax
from jax.sharding import PartitionSpec as P

OWN = 256
VA = 8
VB = 64


def in_one_piece(arrays, axis, split_dim, concat_dim, along):
    widths = [a.shape[along] for a in arrays]
    both = jnp.concatenate(arrays, axis=along)
    filled = lax.all_to_all(both, axis, split_axis=split_dim, concat_axis=concat_dim, tiled=True)
    return tuple(jnp.split(filled, [sum(widths[:k]) for k in range(1, len(widths))], axis=along))


def in_one_piece_2(arrays, axis, split_dim, concat_dim, along):
    widths = [math.prod(a.shape[along:]) for a in arrays]
    both = jnp.concatenate(
        [a.reshape(*a.shape[:along], w) for a, w in zip(arrays, widths)], axis=along
    )
    filled = lax.all_to_all(both, axis, split_axis=split_dim, concat_axis=concat_dim, tiled=True)
    parts = jnp.split(filled, [sum(widths[:k]) for k in range(1, len(widths))], axis=along)
    return tuple(
        (b.reshape(*filled.shape[:along], *a.shape[along:]) for a, b in zip(arrays, parts))
    )


def accumulate(feature_list, voxels, block_rows, block_total):
    slot_count, points = voxels.shape
    group_size = math.gcd(slot_count, 128)
    group_count = slot_count // group_size
    channels = sum_channels(feature_list)
    grouped = tuple((f.reshape((group_count, group_size) + f.shape[1:]) for f in feature_list))
    voxel_groups = voxels.reshape(group_count, group_size, points)
    block_groups = jnp.maximum(block_rows, 0).reshape(group_count, group_size)
    upper_ids = jnp.arange(VA, dtype=jnp.int32)
    lower_ids = jnp.arange(VB, dtype=jnp.int32)

    def fold_group(running, pieces):
        feature_parts, voxel_rows, block_ids = pieces
        features_group = jnp.concatenate(list(feature_parts), axis=1)
        upper_part = voxel_rows // VB
        lower_part = voxel_rows % VB
        chosen = upper_part[:, None, :] == upper_ids[None, :, None]
        left_side = jnp.where(
            chosen[:, None], features_group[:, :, None, :], jnp.zeros((), jnp.bfloat16)
        )
        left_side = left_side.reshape(group_size, channels * VA, points)
        right_side = (lower_part[:, :, None] == lower_ids[None, None, :]).astype(jnp.bfloat16)
        slot_grids = jnp.einsum(
            "gkp,gpb->gkb", left_side, right_side, preferred_element_type=jnp.float32
        )
        slot_grids = slot_grids.reshape(group_size, channels, VA * VB)
        return (running.at[block_ids].add(slot_grids), None)

    running_start = jnp.zeros((block_total, channels, VA * VB), jnp.float32)
    running_end, _ = lax.scan(fold_group, running_start, (grouped, voxel_groups, block_groups))
    return running_end


def sum_channels(feature_list):
    total_channels = 0
    for member in feature_list:
        total_channels = total_channels + member.shape[1]
    return total_channels


def local(
    bin_blocks,
    send_counts,
    voxel_index,
    point_sdf,
    point_weight,
    point_color,
    owner_table,
    old_tsdf,
    old_weight,
):
    owners = lax.axis_size("owner")
    bin_count = bin_blocks.shape[0]
    capacity = 2 * bin_count // owners
    slot_count = owners * capacity
    counts = send_counts[0]
    starts = jnp.cumsum(counts) - counts
    slot_ids = jnp.arange(slot_count, dtype=jnp.int32)
    target = slot_ids // capacity
    position = slot_ids % capacity
    active = position < counts[target]
    source = jnp.clip(starts[target] + position, 0, bin_count - 1)
    blocks_sent = jnp.where(active, owner_table[bin_blocks[source]] % OWN, -1)
    weight = jnp.where(active[:, None], point_weight[source], jnp.zeros((), jnp.bfloat16))
    wide_weight = weight.astype(jnp.float32)
    weighted_sdf = (wide_weight * point_sdf[source].astype(jnp.float32)).astype(jnp.bfloat16)
    geometry = jnp.stack([weight, weighted_sdf], axis=1)
    colors = (wide_weight[:, None, :] * point_color[source].astype(jnp.float32)).astype(
        jnp.bfloat16
    )
    voxels = voxel_index[source]
    replicas = lax.axis_size("rep")
    share = OWN // replicas
    arrived_geometry, arrived_colors, arrived_voxels, arrived_blocks = (
        *in_one_piece((geometry, colors), "owner", 0, 0, 1),
        *in_one_piece_2((voxels, blocks_sent), "owner", 0, 0, 1),
    )
    quota = 2 * bin_count // replicas
    live = arrived_blocks >= 0
    quarter = jnp.where(live, arrived_blocks // share, 0)
    quarter_ids = jnp.arange(replicas, dtype=jnp.int32)
    member = (live[:, None] & (quarter[:, None] == quarter_ids[None, :])).astype(jnp.int32)
    rank = jnp.sum((jnp.cumsum(member, axis=0) - member) * member, axis=1)
    outgoing_slots = replicas * quota
    destination = jnp.where(live, quarter * quota + rank, outgoing_slots).astype(jnp.int32)
    arrived_ids = jnp.arange(arrived_blocks.shape[0], dtype=jnp.int32)
    picked = jnp.zeros((outgoing_slots,), jnp.int32).at[destination].set(arrived_ids, mode="drop")
    filled = jnp.zeros((outgoing_slots,), jnp.bool_).at[destination].set(True, mode="drop")
    send_geometry = jnp.where(
        filled[:, None, None], arrived_geometry[picked], jnp.zeros((), jnp.bfloat16)
    )
    send_colors = jnp.where(
        filled[:, None, None], arrived_colors[picked], jnp.zeros((), jnp.bfloat16)
    )
    send_voxels = arrived_voxels[picked]
    send_places = jnp.where(filled, arrived_blocks[picked] % share, -1).astype(jnp.int32)
    final_geometry, final_colors, final_voxels, final_places = (
        *in_one_piece((send_geometry, send_colors), "rep", 0, 0, 1),
        lax.all_to_all(send_voxels, "rep", split_axis=0, concat_axis=0, tiled=True),
        lax.all_to_all(send_places, "rep", split_axis=0, concat_axis=0, tiled=True),
    )
    cell_sums = accumulate((final_geometry, final_colors), final_voxels, final_places, share)
    geometry_share = cell_sums[:, :2]
    color_share = cell_sums[:, 2:]
    new_weight = old_weight + geometry_share[:, 0]
    joined_sdf = (old_weight * old_tsdf[:, 0] + geometry_share[:, 1]) / new_weight
    joined_color = (old_weight[:, None, :] * old_tsdf[:, 1:] + color_share) / new_weight[:, None, :]
    new_tsdf = jnp.concatenate([joined_sdf[:, None, :], joined_color], axis=1)
    return (new_tsdf, new_weight)


def solution(mesh):
    placed = (
        P(("owner", "rep")),
        P(("owner", "rep"), None),
        P(("owner", "rep"), None),
        P(("owner", "rep"), None),
        P(("owner", "rep"), None),
        P(("owner", "rep"), None, None),
        P(),
        P(("owner", "rep"), None, None),
        P(("owner", "rep"), None),
    )
    return jax.shard_map(
        local,
        mesh=mesh,
        in_specs=placed,
        out_specs=(P(("owner", "rep"), None, None), P(("owner", "rep"), None)),
        check_vma=False,
    )
```

profile of v0, /device:TPU:8, one launch (start us, length us, event | category | flops | bytes accessed | tf_op | source)
XLA Modules:
  0.0 211.6 jit_solution(4263161496959832340)
XLA Ops:
  2.4 3.3 %gather_fusion = s32[512]{0:T(512)S(1)} fusion(s32[128]{0:T(128)S(1)} %bitcast_subtract_fusion, s32[1024]{0:T(1024)S(1)} %pad_clamp_fusion.3), kind=kCustom, calls=%fused_computation | custom fusion | bytes 6144 | tf_op jit(solution)/shard_map/gather | solution.py:92
  5.8 3.5 %gather_fusion.3 = s32[512]{0:T(512)S(1)} fusion(s32[256]{0:T(256)S(1)} %copy-done.2, s32[1024]{0:T(1024)S(1)} %pad_clamp_fusion.2), kind=kCustom, calls=%fused_computation.3 | custom fusion | bytes 6144 | tf_op jit(solution)/shard_map/gather | solution.py:93
  9.4 3.1 %gather_fusion.4 = s32[512]{0:T(512)S(1)} fusion(s32[32768]{0:T(1024)S(1)} %copy-done.3, s32[1024]{0:T(1024)S(1)} %pad_clamp_fusion.1), kind=kCustom, calls=%fused_computation.4 | custom fusion | bytes 6144 | tf_op jit(solution)/shard_map/gather | solution.py:93
  12.7 3.3 %gather_fusion.2 = s32[512]{0:T(512)S(1)} fusion(s32[128]{0:T(128)S(1)} %bitcast.122, s32[1024]{0:T(1024)S(1)} %pad_clamp_fusion.3), kind=kCustom, calls=%fused_computation.2 | custom fusion | bytes 6144 | tf_op jit(solution)/shard_map/gather | solution.py:91
  16.2 0.9 copy.43
  17.1 1.0 gather_fusion.1
  18.2 0.9 pad_add_fusion
  19.1 17.4 %all-to-all-start = ((s32[128,4,129]{2,1,0:T(4,128)}), s32[128,4,129]{2,1,0:T(4,128)S(1)}, u32[]{:S(2)}, u32[]{:S(2)}) async-start(s32[128,4,129]{2,1,0:T(4,128)} %pad_add_fusion), calls=%async_computation | async-start | bytes 1048576 | tf_op jit(solution)/shard_map/all_to_all | solution.py:24
  36.5 1.3 gather_fusion.7
  37.8 1.3 gather_fusion.8
  39.2 2.7 %gather_fusion.9 = bf16[512,3,128]{2,0,1:T(8,128)(2,1)S(1)} fusion(bf16[256,3,128]{2,0,1:T(8,128)(2,1)S(1)} %copy-done, s32[1024]{0:T(1024)S(1)} %pad_clamp_fusion.2), kind=kCustom, calls=%fused_computation.9 | custom fusion | bytes 788480 | tf_op jit(solution)/shard_map/gather | solution.py:98
  42.4 1.5 copy.45
  43.8 12.9 %all-to-all-done = s32[128,4,129]{2,1,0:T(4,128)S(1)} async-done(((s32[128,4,129]{2,1,0:T(4,128)}), s32[128,4,129]{2,1,0:T(4,128)S(1)}, u32[]{:S(2)}, u32[]{:S(2)}) %all-to-all-start) | async-done | bytes 264224 | tf_op jit(solution)/shard_map/all_to_all | solution.py:24
  56.7 6.5 %all-to-all-start.3 = ((bf16[512,5,128]{2,1,0:T(8,128)(2,1)}), bf16[512,5,128]{2,1,0:T(8,128)(2,1)S(1)}, u32[]{:S(2)}, u32[]{:S(2)}) async-start(bf16[512,5,128]{2,1,0:T(8,128)(2,1)} %copy.45), calls=%async_computation.3 | async-start | bytes 2097152 | tf_op jit(solution)/shard_map/all_to_all | solution.py:15
  63.7 1.2 reduce-window.20
  65.4 2.6 %scatter_custom_fusion.2 = s32[512]{0:T(512)S(1)} fusion(s32[512]{0:T(512)S(1)} %bitcast.136, s32[512]{0:T(512)S(1)} %iota.48, s32[]{:T(128)} %copy.70), kind=kCustom, calls=%fused_computation.118 | custom fusion | bytes 2052 | tf_op jit(solution)/shard_map/scatter | solution.py:117
  68.1 2.4 %scatter_custom_fusion.1 = pred[512]{0:T(512)(128)(4,1)S(1)} fusion(s32[512]{0:T(512)S(1)} %bitcast.137, pred[512]{0:T(512)(128)(4,1)S(1)} %broadcast.498, pred[]{:T(512)} %constant.145.clone.1), kind=kCustom, calls=%fused_computation.122 | custom fusion | bytes 513 | tf_op jit(solution)/shard_map/scatter | solution.py:118
  70.5 3.5 %gather_fusion.5 = s32[512]{0:T(512)S(1)} fusion(s32[512]{0:T(512)S(1)} %bitcast.123, s32[1024]{0:T(1024)S(1)} %pad_clamp_fusion), kind=kCustom, calls=%fused_computation.5 | custom fusion | bytes 6144 | tf_op jit(solution)/shard_map/gather | solution.py:126
  74.6 20.1 %all-to-all-done.3 = bf16[512,5,128]{2,1,0:T(8,128)(2,1)S(1)} async-done(((bf16[512,5,128]{2,1,0:T(8,128)(2,1)}), bf16[512,5,128]{2,1,0:T(8,128)(2,1)S(1)}, u32[]{:S(2)}, u32[]{:S(2)}) %all-to-all-start.3) | async-done | bytes 655392 | tf_op jit(solution)/shard_map/all_to_all | solution.py:15
  94.7 4.3 %all-to-all-start.1 = ((s32[4,128,1]{1,2,0:T(1,128)}), s32[4,128,1]{1,2,0:T(1,128)S(1)}, u32[]{:S(2)}, u32[]{:S(2)}) async-start(s32[4,128,1]{1,2,0:T(1,128)} %bitcast.15), calls=%async_computation.1 | async-start | bytes 4096 | tf_op jit(solution)/shard_map/all_to_all | solution.py:130
  99.2 2.1 gather_fusion.10
  101.3 1.8 broadcast_select_fusion.1
  103.3 2.1 gather_fusion.11
  105.4 1.8 broadcast_select_fusion
  107.2 1.5 pad_maximum_fusion.1
  108.7 4.8 %all-to-all-start.4 = ((bf16[512,5,128]{2,1,0:T(8,128)(2,1)}), bf16[512,5,128]{2,1,0:T(8,128)(2,1)S(1)}, u32[]{:S(2)}, u32[]{:S(2)}) async-start(bf16[512,5,128]{2,1,0:T(8,128)(2,1)} %pad_maximum_fusion.1), calls=%async_computation.4 | async-start | bytes 2097152 | tf_op jit(solution)/shard_map/all_to_all | solution.py:15
  113.5 1.6 gather_fusion.6
  115.2 11.3 %all-to-all-done.4 = bf16[512,5,128]{2,1,0:T(8,128)(2,1)S(1)} async-done(((bf16[512,5,128]{2,1,0:T(8,128)(2,1)}), bf16[512,5,128]{2,1,0:T(8,128)(2,1)S(1)}, u32[]{:S(2)}, u32[]{:S(2)}) %all-to-all-start.4) | async-done | bytes 655392 | tf_op jit(solution)/shard_map/all_to_all | solution.py:15
  126.5 4.0 %all-to-all-start.2 = ((s32[4,128,128]{2,1,0:T(8,128)}), s32[4,128,128]{2,1,0:T(8,128)}, u32[]{:S(2)}, u32[]{:S(2)}) async-start(s32[4,128,128]{2,1,0:T(8,128)} %bitcast.17), calls=%async_computation.2 | async-start | bytes 524288 | tf_op jit(solution)/shard_map/all_to_all | solution.py:129
  130.6 1.1 split.29
  132.5 4.8 %all-to-all-done.2 = s32[4,128,128]{2,1,0:T(8,128)} async-done(((s32[4,128,128]{2,1,0:T(8,128)}), s32[4,128,128]{2,1,0:T(8,128)}, u32[]{:S(2)}, u32[]{:S(2)}) %all-to-all-start.2) | async-done | bytes 262176 | tf_op jit(solution)/shard_map/all_to_all | solution.py:129
  137.5 71.1 %while.13 = (s32[]{:T(128)}, f32[64,5,512]{2,1,0:T(8,128)S(1)}, s32[4,128]{1,0:T(4,128)S(1)}, s32[4,128,128]{2,1,0:T(8,128)}, bf16[4,128,2,128]{3,2,1,0:T(2,128)...) while((s32[]{:T(128)}, f32[64,5,512]{2,1,0:T(8,128)S(1)}, s32[4,128]{1,0:T(4,128)S(1)}, ...), condition=%wide.region_8.9_spmd.clone, body=%wide.region_6.8_spmd.clone.sunk | while | flops 86786432 | bytes 11994721 | solution.py:60
  137.5 0.9 add_select_fusion.8
  138.4 0.9 add_select_fusion.9
  139.3 1.0 dynamic-slice_bitcast_fusion.4
  140.2 0.9 dynamic-slice_bitcast_fusion.5
  141.4 2.8 %fusion.53 = f32[128,40,64]{2,1,0:T(8,128)} fusion(s32[128,128]{1,0:T(8,128)S(1)} %add_select_fusion.9, pred[128,8,128]{2,1,0:T(8,128)(4,1)S(1)} %iota_compare_fusion.8, bf16[128,5,128]{2,1,0:T(8,128)(2,1)S(1)} %pad_maximum_fusion.5), kind=kOutput, calls=%fused_computation.18.clone.1 | convolution fusion | flops 85590016 | bytes 1671168 | tf_op jit(solution)/shard_map/while/body/eval_jaxpr/gkp,gpb->gkb/dot_general | solution.py:53
  144.1 3.2 %copy.60 = f32[128,40,64]{0,2,1:T(8,128)} copy(f32[128,40,64]{2,1,0:T(8,128)} %fusion.53) | data formatting | bytes 2621440 | tf_op jit(solution)/shard_map/while/body/eval_jaxpr/gkp,gpb->gkb/dot_general | solution.py:53
  147.3 2.1 %copy.61 = f32[128,5,512]{2,1,0:T(8,128)S(1)} copy(f32[128,5,512]{0,2,1:T(8,128)} %bitcast.124) | data formatting | bytes 2621440 | tf_op jit(solution)/shard_map/while/body/eval_jaxpr/reshape | solution.py:56
  149.4 5.8 %scatter_fusion = f32[64,5,512]{2,1,0:T(8,128)S(1)} fusion(f32[64,5,512]{2,1,0:T(8,128)S(1)} %get-tuple-element.189, s32[128]{0:T(128)S(1)} %fusion.52, f32[128,5,512]{2,1,0:T(8,128)S(1)} %copy.61), kind=kCustom, calls=%fused_computation.12.clone.clone.1 | custom fusion | flops 327680 | bytes 3932672 | tf_op jit(solution)/shard_map/while/body/eval_jaxpr/scatter-add | solution.py:57
  155.3 0.9 add_select_fusion.8
  156.2 0.9 add_select_fusion.9
  157.1 1.0 dynamic-slice_bitcast_fusion.4
  158.0 0.9 dynamic-slice_bitcast_fusion.5
  159.1 2.8 %fusion.53 = f32[128,40,64]{2,1,0:T(8,128)} fusion(s32[128,128]{1,0:T(8,128)S(1)} %add_select_fusion.9, pred[128,8,128]{2,1,0:T(8,128)(4,1)S(1)} %iota_compare_fusion.8, bf16[128,5,128]{2,1,0:T(8,128)(2,1)S(1)} %pad_maximum_fusion.5), kind=kOutput, calls=%fused_computation.18.clone.1 | convolution fusion | flops 85590016 | bytes 1671168 | tf_op jit(solution)/shard_map/while/body/eval_jaxpr/gkp,gpb->gkb/dot_general | solution.py:53
  161.9 3.2 %copy.60 = f32[128,40,64]{0,2,1:T(8,128)} copy(f32[128,40,64]{2,1,0:T(8,128)} %fusion.53) | data formatting | bytes 2621440 | tf_op jit(solution)/shard_map/while/body/eval_jaxpr/gkp,gpb->gkb/dot_general | solution.py:53
  165.1 2.1 %copy.61 = f32[128,5,512]{2,1,0:T(8,128)S(1)} copy(f32[128,5,512]{0,2,1:T(8,128)} %bitcast.124) | data formatting | bytes 2621440 | tf_op jit(solution)/shard_map/while/body/eval_jaxpr/reshape | solution.py:56
  167.2 5.8 %scatter_fusion = f32[64,5,512]{2,1,0:T(8,128)S(1)} fusion(f32[64,5,512]{2,1,0:T(8,128)S(1)} %get-tuple-element.189, s32[128]{0:T(128)S(1)} %fusion.52, f32[128,5,512]{2,1,0:T(8,128)S(1)} %copy.61), kind=kCustom, calls=%fused_computation.12.clone.clone.1 | custom fusion | flops 327680 | bytes 3932672 | tf_op jit(solution)/shard_map/while/body/eval_jaxpr/scatter-add | solution.py:57
  173.1 0.9 add_select_fusion.8
  174.8 1.0 dynamic-slice_bitcast_fusion.4
  175.8 0.9 dynamic-slice_bitcast_fusion.5
  176.9 2.8 %fusion.53 = f32[128,40,64]{2,1,0:T(8,128)} fusion(s32[128,128]{1,0:T(8,128)S(1)} %add_select_fusion.9, pred[128,8,128]{2,1,0:T(8,128)(4,1)S(1)} %iota_compare_fusion.8, bf16[128,5,128]{2,1,0:T(8,128)(2,1)S(1)} %pad_maximum_fusion.5), kind=kOutput, calls=%fused_computation.18.clone.1 | convolution fusion | flops 85590016 | bytes 1671168 | tf_op jit(solution)/shard_map/while/body/eval_jaxpr/gkp,gpb->gkb/dot_general | solution.py:53
  179.7 3.2 %copy.60 = f32[128,40,64]{0,2,1:T(8,128)} copy(f32[128,40,64]{2,1,0:T(8,128)} %fusion.53) | data formatting | bytes 2621440 | tf_op jit(solution)/shard_map/while/body/eval_jaxpr/gkp,gpb->gkb/dot_general | solution.py:53
  182.8 2.1 %copy.61 = f32[128,5,512]{2,1,0:T(8,128)S(1)} copy(f32[128,5,512]{0,2,1:T(8,128)} %bitcast.124) | data formatting | bytes 2621440 | tf_op jit(solution)/shard_map/while/body/eval_jaxpr/reshape | solution.py:56
  185.0 5.8 %scatter_fusion = f32[64,5,512]{2,1,0:T(8,128)S(1)} fusion(f32[64,5,512]{2,1,0:T(8,128)S(1)} %get-tuple-element.189, s32[128]{0:T(128)S(1)} %fusion.52, f32[128,5,512]{2,1,0:T(8,128)S(1)} %copy.61), kind=kCustom, calls=%fused_computation.12.clone.clone.1 | custom fusion | flops 327680 | bytes 3932672 | tf_op jit(solution)/shard_map/while/body/eval_jaxpr/scatter-add | solution.py:57
  190.8 0.9 add_select_fusion.8
  192.6 1.0 dynamic-slice_bitcast_fusion.4
  193.6 0.9 dynamic-slice_bitcast_fusion.5
  194.7 2.8 %fusion.53 = f32[128,40,64]{2,1,0:T(8,128)} fusion(s32[128,128]{1,0:T(8,128)S(1)} %add_select_fusion.9, pred[128,8,128]{2,1,0:T(8,128)(4,1)S(1)} %iota_compare_fusion.8, bf16[128,5,128]{2,1,0:T(8,128)(2,1)S(1)} %pad_maximum_fusion.5), kind=kOutput, calls=%fused_computation.18.clone.1 | convolution fusion | flops 85590016 | bytes 1671168 | tf_op jit(solution)/shard_map/while/body/eval_jaxpr/gkp,gpb->gkb/dot_general | solution.py:53
  197.4 3.2 %copy.60 = f32[128,40,64]{0,2,1:T(8,128)} copy(f32[128,40,64]{2,1,0:T(8,128)} %fusion.53) | data formatting | bytes 2621440 | tf_op jit(solution)/shard_map/while/body/eval_jaxpr/gkp,gpb->gkb/dot_general | solution.py:53
  200.6 2.1 %copy.61 = f32[128,5,512]{2,1,0:T(8,128)S(1)} copy(f32[128,5,512]{0,2,1:T(8,128)} %bitcast.124) | data formatting | bytes 2621440 | tf_op jit(solution)/shard_map/while/body/eval_jaxpr/reshape | solution.py:56
  202.7 5.8 %scatter_fusion = f32[64,5,512]{2,1,0:T(8,128)S(1)} fusion(f32[64,5,512]{2,1,0:T(8,128)S(1)} %get-tuple-element.189, s32[128]{0:T(128)S(1)} %fusion.52, f32[128,5,512]{2,1,0:T(8,128)S(1)} %copy.61), kind=kCustom, calls=%fused_computation.12.clone.clone.1 | custom fusion | flops 327680 | bytes 3932672 | tf_op jit(solution)/shard_map/while/body/eval_jaxpr/scatter-add | solution.py:57
  209.0 0.9 fusion.21
  210.5 1.0 pad_maximum_fusion.3
  (80 shorter events, 9.0 us)
Async XLA Ops:
  0.6 38.5 %copy-start = (bf16[256,3,128]{2,0,1:T(8,128)(2,1)S(1)}, bf16[256,3,128]{2,0,1:T(8,128)(2,1)}, u32[]{:S(2)}) copy-start(bf16[256,3,128]{2,0,1:T(8,128)(2,1)} %param.16) | copy-start | bytes 589828
  0.6 5.2 %copy-start.2 = (s32[256]{0:T(256)S(1)}, s32[256]{0:T(256)}, u32[]{:S(2)}) copy-start(s32[256]{0:T(256)} %param.11) | copy-start | bytes 3076
  2.4 7.0 %copy-start.3 = (s32[32768]{0:T(1024)S(1)}, s32[32768]{0:T(1024)}, u32[]{:S(2)}) copy-start(s32[32768]{0:T(1024)} %param.17) | copy-start | bytes 393220
  5.8 6.8 %copy-start.1 = (s32[1,128]{1,0:T(1,128)S(1)}, s32[1,128]{1,0:T(1,128)}, u32[]{:S(2)}) copy-start(s32[1,128]{1,0:T(1,128)} %param.12) | copy-start | bytes 1540
  9.4 7.7 %copy-start.4 = (s32[256,128]{1,0:T(8,128)S(1)}, s32[256,128]{1,0:T(8,128)}, u32[]{:S(2)}) copy-start(s32[256,128]{1,0:T(8,128)} %param.13) | copy-start | bytes 393220
  17.1 19.4 %copy-start.5 = (bf16[256,128]{1,0:T(8,128)(2,1)S(1)}, bf16[256,128]{1,0:T(8,128)(2,1)}, u32[]{:S(2)}) copy-start(bf16[256,128]{1,0:T(8,128)(2,1)} %param.15) | copy-start | bytes 196612
  18.1 19.7 %copy-start.6 = (bf16[256,128]{1,0:T(8,128)(2,1)S(1)}, bf16[256,128]{1,0:T(8,128)(2,1)}, u32[]{:S(2)}) copy-start(bf16[256,128]{1,0:T(8,128)(2,1)} %param.14) | copy-start | bytes 196612
  19.1 37.7 %all-to-all-start = ((s32[128,4,129]{2,1,0:T(4,128)}), s32[128,4,129]{2,1,0:T(4,128)S(1)}, u32[]{:S(2)}, u32[]{:S(2)}) async-start(s32[128,4,129]{2,1,0:T(4,128)} %pad_add_fusion), calls=%async_computation | async-start | bytes 1048576 | tf_op jit(solution)/shard_map/all_to_all | solution.py:24
  56.7 37.9 %all-to-all-start.3 = ((bf16[512,5,128]{2,1,0:T(8,128)(2,1)}), bf16[512,5,128]{2,1,0:T(8,128)(2,1)S(1)}, u32[]{:S(2)}, u32[]{:S(2)}) async-start(bf16[512,5,128]{2,1,0:T(8,128)(2,1)} %copy.45), calls=%async_computation.3 | async-start | bytes 2097152 | tf_op jit(solution)/shard_map/all_to_all | solution.py:15
  94.7 14.0 %all-to-all-start.1 = ((s32[4,128,1]{1,2,0:T(1,128)}), s32[4,128,1]{1,2,0:T(1,128)S(1)}, u32[]{:S(2)}, u32[]{:S(2)}) async-start(s32[4,128,1]{1,2,0:T(1,128)} %bitcast.15), calls=%async_computation.1 | async-start | bytes 4096 | tf_op jit(solution)/shard_map/all_to_all | solution.py:130
  108.7 17.8 %all-to-all-start.4 = ((bf16[512,5,128]{2,1,0:T(8,128)(2,1)}), bf16[512,5,128]{2,1,0:T(8,128)(2,1)S(1)}, u32[]{:S(2)}, u32[]{:S(2)}) async-start(bf16[512,5,128]{2,1,0:T(8,128)(2,1)} %pad_maximum_fusion.1), calls=%async_computation.4 | async-start | bytes 2097152 | tf_op jit(solution)/shard_map/all_to_all | solution.py:15
  126.5 10.8 %all-to-all-start.2 = ((s32[4,128,128]{2,1,0:T(8,128)}), s32[4,128,128]{2,1,0:T(8,128)}, u32[]{:S(2)}, u32[]{:S(2)}) async-start(s32[4,128,128]{2,1,0:T(8,128)} %bitcast.17), calls=%async_computation.2 | async-start | bytes 524288 | tf_op jit(solution)/shard_map/all_to_all | solution.py:129
  137.4 71.6 %slice-start = ((f32[64,4,512]{2,1,0:T(4,128)}), f32[64,1,512]{2,1,0:T(1,128)S(1)}, s32[]{:S(2)}) async-start(f32[64,4,512]{2,1,0:T(4,128)} %param.18), calls=%async_computation.5 | async-start | bytes 262144 | tf_op jit(solution)/shard_map/slice | solution.py:136
  208.6 1.4 copy-start.7
  208.6 1.4 copy-start.8
  210.0 1.6 copy-start.9
where the time goes:
time: 213 us; the launch traced here: 212 us
  local copies, waits for them, and re-layouts  69.7 us (33%)
  waiting for transfers between devices  49.1 us (23%)
  other arithmetic  43.3 us (20%)
  starting transfers between devices  37 us (17%)
  matrix products  11 us (5%)
    all_to_all x2, waiting for transfers between devices, in_one_piece(): lax.all_to_all(both, axis, split_axis=split_dim, concat_axis=concat_dim,...  31.4 us
    scatter-add x4, other arithmetic, fold_group(): return (running.at[block_ids].add(slot_grids), None)  23.4 us
    all_to_all x1, starting transfers between devices, in_one_piece_2(): lax.all_to_all(both, axis, split_axis=split_dim, concat_axis=concat_dim,...  17.4 us
    all_to_all x1, waiting for transfers between devices, in_one_piece_2(): lax.all_to_all(both, axis, split_axis=split_dim, concat_axis=concat_dim,...  12.9 us
    dot_general x4, local copies, waits for them, and re-layouts, fold_group(): jnp.einsum('gkp,gpb->gkb', left_side, right_side, preferred_element_type=...  12.6 us
    all_to_all x2, starting transfers between devices, in_one_piece(): lax.all_to_all(both, axis, split_axis=split_dim, concat_axis=concat_dim,...  11.3 us
    dot_general x4, matrix products, fold_group(): jnp.einsum('gkp,gpb->gkb', left_side, right_side, preferred_element_type=...  11 us
    reshape x4, local copies, waits for them, and re-layouts, fold_group(): slot_grids = slot_grids.reshape(group_size, channels, VA * VB)  8.49 us
  transfers between devices with their start and end apart: 5, of which 4 were waited for; matrix products, arithmetic and copies ran while one was open for 15% of the time, Pallas kernels for 0%

commit v1 on v0

--- a/solution.py
+++ b/solution.py
@@ -7,6 +7,28 @@
 OWN = 256
 VA = 8
 VB = 64
+
+
+def in_blocks(value, dim, size):
+    before, after = (value.shape[:dim], value.shape[dim + 1 :])
+    return jnp.moveaxis(value.reshape(*before, size, -1, *after), dim, 0)
+
+
+def laid_out(tiles, dim):
+    tiles = jnp.moveaxis(tiles, 0, dim)
+    shape = tiles.shape
+    return tiles.reshape(*shape[:dim], shape[dim] * shape[dim + 1], *shape[dim + 2 :])
+
+
+def rotated_exchange(x, axis, split_dim, concat_dim):
+    count, index = (lax.axis_size(axis), lax.axis_index(axis))
+    blocks = in_blocks(x, split_dim, count)
+    finished = [blocks[index]]
+    for step in range(1, count):
+        sent = blocks[(index + step) % count]
+        finished.append(lax.ppermute(sent, axis, [(i, (i + step) % count) for i in range(count)]))
+    blocks = jnp.stack(finished)[(index - jnp.arange(count)) % count]
+    return laid_out(blocks, concat_dim)
 
 
 def in_one_piece(arrays, axis, split_dim, concat_dim, along):
@@ -127,7 +149,7 @@
     final_geometry, final_colors, final_voxels, final_places = (
         *in_one_piece((send_geometry, send_colors), "rep", 0, 0, 1),
         lax.all_to_all(send_voxels, "rep", split_axis=0, concat_axis=0, tiled=True),
-        lax.all_to_all(send_places, "rep", split_axis=0, concat_axis=0, tiled=True),
+        rotated_exchange(send_places, "rep", 0, 0),
     )
     cell_sums = accumulate((final_geometry, final_colors), final_voxels, final_places, share)
     geometry_share = cell_sums[:, :2]

time: 213 us -> 210 us (0.986)
  the two profiles are of different devices: /device:TPU:8 before, /device:TPU:24 now
where the time goes in v1:
time: 210 us; the launch traced here: 208 us
  local copies, waits for them, and re-layouts  70.3 us (33%)
  starting transfers between devices  45.9 us (22%)
  other arithmetic  42.7 us (20%)
  waiting for transfers between devices  36.9 us (18%)
  matrix products  11.1 us (5%)
    scatter-add x4, other arithmetic, fold_group(): return (running.at[block_ids].add(slot_grids), None)  23.3 us
    all_to_all x2, waiting for transfers between devices, in_one_piece(): lax.all_to_all(both, axis, split_axis=split_dim, concat_axis=concat_dim,...  17.8 us
    all_to_all x1, starting transfers between devices, in_one_piece_2(): lax.all_to_all(both, axis, split_axis=split_dim, concat_axis=concat_dim,...  17.3 us
    all_to_all x2, starting transfers between devices, in_one_piece(): lax.all_to_all(both, axis, split_axis=split_dim, concat_axis=concat_dim,...  12.6 us
    dot_general x4, local copies, waits for them, and re-layouts, fold_group(): jnp.einsum('gkp,gpb->gkb', left_side, right_side, preferred_element_type=...  12.6 us
    ppermute x3, starting transfers between devices, rotated_exchange(): lax.ppermute(sent, axis, [(i, (i + step) % count) for i in range(count)])  11.9 us
    dot_general x4, matrix products, fold_group(): jnp.einsum('gkp,gpb->gkb', left_side, right_side, preferred_element_type=...  11.1 us
    all_to_all x1, waiting for transfers between devices, in_one_piece_2(): lax.all_to_all(both, axis, split_axis=split_dim, concat_axis=concat_dim,...  11 us
  transfers between devices with their start and end apart: 7, of which 4 were waited for; matrix products, arithmetic and copies ran while one was open for 11% of the time, Pallas kernels for 0%

profile of v1, /device:TPU:24, one launch (start us, length us, event | category | flops | bytes accessed | tf_op | source)
XLA Modules:
  0.0 208.4 jit_solution(14428638364156429713)
XLA Ops:
  2.4 3.3 %gather_fusion = s32[512]{0:T(512)S(1)} fusion(s32[128]{0:T(128)S(1)} %bitcast_subtract_fusion, s32[1024]{0:T(1024)S(1)} %pad_clamp_fusion.4), kind=kCustom, calls=%fused_computation | custom fusion | bytes 6144 | tf_op jit(solution)/shard_map/gather | solution.py:114
  5.9 3.3 %gather_fusion.2 = s32[512]{0:T(512)S(1)} fusion(s32[128]{0:T(128)S(1)} %bitcast.133, s32[1024]{0:T(1024)S(1)} %pad_clamp_fusion.4), kind=kCustom, calls=%fused_computation.2 | custom fusion | bytes 6144 | tf_op jit(solution)/shard_map/gather | solution.py:113
  9.2 3.5 %gather_fusion.3 = s32[512]{0:T(512)S(1)} fusion(s32[256]{0:T(256)S(1)} %copy-done.2, s32[1024]{0:T(1024)S(1)} %pad_clamp_fusion.3), kind=kCustom, calls=%fused_computation.3 | custom fusion | bytes 6144 | tf_op jit(solution)/shard_map/gather | solution.py:115
  12.8 3.1 %gather_fusion.4 = s32[512]{0:T(512)S(1)} fusion(s32[32768]{0:T(1024)S(1)} %copy-done.3, s32[1024]{0:T(1024)S(1)} %pad_clamp_fusion.2), kind=kCustom, calls=%fused_computation.4 | custom fusion | bytes 6144 | tf_op jit(solution)/shard_map/gather | solution.py:115
  16.2 0.9 copy.43
  17.1 1.0 gather_fusion.1
  18.2 0.9 pad_add_fusion
  19.1 17.3 %all-to-all-start = ((s32[128,4,129]{2,1,0:T(4,128)}), s32[128,4,129]{2,1,0:T(4,128)S(1)}, u32[]{:S(2)}, u32[]{:S(2)}) async-start(s32[128,4,129]{2,1,0:T(4,128)} %pad_add_fusion), calls=%async_computation | async-start | bytes 1048576 | tf_op jit(solution)/shard_map/all_to_all | solution.py:46
  36.4 1.3 gather_fusion.8
  37.8 1.3 gather_fusion.9
  39.5 2.7 %gather_fusion.10 = bf16[512,3,128]{2,0,1:T(8,128)(2,1)S(1)} fusion(bf16[256,3,128]{2,0,1:T(8,128)(2,1)S(1)} %copy-done, s32[1024]{0:T(1024)S(1)} %pad_clamp_fusion.3), kind=kCustom, calls=%fused_computation.10 | custom fusion | bytes 788480 | tf_op jit(solution)/shard_map/gather | solution.py:120
  42.4 1.5 copy.45
  43.9 11.0 %all-to-all-done = s32[128,4,129]{2,1,0:T(4,128)S(1)} async-done(((s32[128,4,129]{2,1,0:T(4,128)}), s32[128,4,129]{2,1,0:T(4,128)S(1)}, u32[]{:S(2)}, u32[]{:S(2)}) %all-to-all-start) | async-done | bytes 264224 | tf_op jit(solution)/shard_map/all_to_all | solution.py:46
  54.9 8.3 %all-to-all-start.2 = ((bf16[512,5,128]{2,1,0:T(8,128)(2,1)}), bf16[512,5,128]{2,1,0:T(8,128)(2,1)S(1)}, u32[]{:S(2)}, u32[]{:S(2)}) async-start(bf16[512,5,128]{2,1,0:T(8,128)(2,1)} %copy.45), calls=%async_computation.2 | async-start | bytes 2097152 | tf_op jit(solution)/shard_map/all_to_all | solution.py:37
  63.7 1.2 reduce-window.20
  65.4 2.6 %scatter_custom_fusion.2 = s32[512]{0:T(512)S(1)} fusion(s32[512]{0:T(512)S(1)} %bitcast.147, s32[512]{0:T(512)S(1)} %iota.52, s32[]{:T(128)} %copy.70), kind=kCustom, calls=%fused_computation.126 | custom fusion | bytes 2052 | tf_op jit(solution)/shard_map/scatter | solution.py:139
  68.1 2.4 %scatter_custom_fusion.1 = pred[512]{0:T(512)(128)(4,1)S(1)} fusion(s32[512]{0:T(512)S(1)} %bitcast.148, pred[512]{0:T(512)(128)(4,1)S(1)} %broadcast.566, pred[]{:T(512)} %constant.175.clone.1), kind=kCustom, calls=%fused_computation.134 | custom fusion | bytes 513 | tf_op jit(solution)/shard_map/scatter | solution.py:140
  70.5 3.5 %gather_fusion.5 = s32[512]{0:T(512)S(1)} fusion(s32[512]{0:T(512)S(1)} %bitcast.134, s32[1024]{0:T(1024)S(1)} %pad_clamp_fusion.1), kind=kCustom, calls=%fused_computation.5 | custom fusion | bytes 6144 | tf_op jit(solution)/shard_map/gather | solution.py:148
  74.0 17.8 %all-to-all-done.2 = bf16[512,5,128]{2,1,0:T(8,128)(2,1)S(1)} async-done(((bf16[512,5,128]{2,1,0:T(8,128)(2,1)}), bf16[512,5,128]{2,1,0:T(8,128)(2,1)S(1)}, u32[]{:S(2)}, u32[]{:S(2)}) %all-to-all-start.2) | async-done | bytes 655392 | tf_op jit(solution)/shard_map/all_to_all | solution.py:37
  92.0 2.1 %gather_fusion.11 = bf16[512,2,128]{2,1,0:T(2,128)(2,1)S(1)} fusion(bf16[512,2,128]{2,1,0:T(2,128)(2,1)S(1)} %split.26, s32[1024]{0:T(1024)S(1)} %pad_clamp_fusion.1), kind=kCustom, calls=%fused_computation.11 | custom fusion | bytes 526336 | tf_op jit(solution)/shard_map/gather | solution.py:142
  94.4 2.1 gather_fusion.12
  96.5 1.8 broadcast_select_fusion.1
  98.3 1.8 broadcast_select_fusion
  100.0 1.5 pad_maximum_fusion.1
  101.6 4.3 %all-to-all-start.3 = ((bf16[512,5,128]{2,1,0:T(8,128)(2,1)}), bf16[512,5,128]{2,1,0:T(8,128)(2,1)S(1)}, u32[]{:S(2)}, u32[]{:S(2)}) async-start(bf16[512,5,128]{2,1,0:T(8,128)(2,1)} %pad_maximum_fusion.1), calls=%async_computation.3 | async-start | bytes 2097152 | tf_op jit(solution)/shard_map/all_to_all | solution.py:37
  105.9 3.9 %collective-permute-start = (s32[128]{0:T(128)S(1)}, s32[128]{0:T(128)S(1)}, u32[]{:S(2)}, u32[]{:S(2)}) collective-permute-start(s32[128]{0:T(128)S(1)} %get-tuple-element.143), channel_id=1, source_target_pairs={{0,1},{1,2},{2,3},{3,0},{4,5},{5,6},{6,7},{7,4},{8,9},{9,10},{10,1... | collective-permute-start | bytes 1544 | tf_op jit(solution)/shard_map/ppermute | solution.py:29
  109.8 4.6 %collective-permute-start.1 = (s32[128]{0:T(128)S(1)}, s32[128]{0:T(128)S(1)}, u32[]{:S(2)}, u32[]{:S(2)}) collective-permute-start(s32[128]{0:T(128)S(1)} %get-tuple-element.142), channel_id=1, source_target_pairs={{0,2},{1,3},{2,0},{3,1},{4,6},{5,7},{6,4},{7,5},{8,10},{9,11},{10,... | collective-permute-start | bytes 1544 | tf_op jit(solution)/shard_map/ppermute | solution.py:29
  114.4 3.4 %collective-permute-start.2 = (s32[128]{0:T(128)S(1)}, s32[128]{0:T(128)S(1)}, u32[]{:S(2)}, u32[]{:S(2)}) collective-permute-start(s32[128]{0:T(128)S(1)} %get-tuple-element.141), channel_id=1, source_target_pairs={{0,3},{1,0},{2,1},{3,2},{4,7},{5,4},{6,5},{7,6},{8,11},{9,8},{10,9... | collective-permute-start | bytes 1544 | tf_op jit(solution)/shard_map/ppermute | solution.py:29
  117.8 1.7 gather_fusion.7
  119.5 2.9 %collective-permute-done.1 = s32[128]{0:T(128)S(1)} collective-permute-done((s32[128]{0:T(128)S(1)}, s32[128]{0:T(128)S(1)}, u32[]{:S(2)}, u32[]{:S(2)}) %collective-permute-start.1) | collective-permute-done | bytes 544 | tf_op jit(solution)/shard_map/ppermute | solution.py:29
  123.0 4.0 %all-to-all-start.1 = ((s32[4,128,128]{2,1,0:T(8,128)}), s32[4,128,128]{2,1,0:T(8,128)}, u32[]{:S(2)}, u32[]{:S(2)}) async-start(s32[4,128,128]{2,1,0:T(8,128)} %bitcast.23), calls=%async_computation.1 | async-start | bytes 524288 | tf_op jit(solution)/shard_map/all_to_all | solution.py:151
  127.0 1.1 split.29
  129.0 5.2 %all-to-all-done.1 = s32[4,128,128]{2,1,0:T(8,128)} async-done(((s32[4,128,128]{2,1,0:T(8,128)}), s32[4,128,128]{2,1,0:T(8,128)}, u32[]{:S(2)}, u32[]{:S(2)}) %all-to-all-start.1) | async-done | bytes 262176 | tf_op jit(solution)/shard_map/all_to_all | solution.py:151
  134.3 71.2 %while.13 = (s32[]{:T(128)}, f32[64,5,512]{2,1,0:T(8,128)S(1)}, s32[4,128]{1,0:T(4,128)S(1)}, s32[4,128,128]{2,1,0:T(8,128)}, bf16[4,128,2,128]{3,2,1,0:T(2,128)...) while((s32[]{:T(128)}, f32[64,5,512]{2,1,0:T(8,128)S(1)}, s32[4,128]{1,0:T(4,128)S(1)}, ...), condition=%wide.region_8.9_spmd.clone, body=%wide.region_6.8_spmd.clone.sunk | while | flops 86786432 | bytes 11994721 | solution.py:82
  134.3 0.9 add_select_fusion.8
  136.1 1.0 dynamic-slice_bitcast_fusion.4
  137.1 0.9 dynamic-slice_bitcast_fusion.5
  138.2 2.8 %fusion.59 = f32[128,40,64]{2,1,0:T(8,128)} fusion(s32[128,128]{1,0:T(8,128)S(1)} %add_select_fusion.9, pred[128,8,128]{2,1,0:T(8,128)(4,1)S(1)} %iota_compare_fusion.8, bf16[128,5,128]{2,1,0:T(8,128)(2,1)S(1)} %pad_maximum_fusion.5), kind=kOutput, calls=%fused_computation.19.clone.1 | convolution fusion | flops 85590016 | bytes 1671168 | tf_op jit(solution)/shard_map/while/body/eval_jaxpr/gkp,gpb->gkb/dot_general | solution.py:75
  141.0 3.1 %copy.60 = f32[128,40,64]{0,2,1:T(8,128)} copy(f32[128,40,64]{2,1,0:T(8,128)} %fusion.59) | data formatting | bytes 2621440 | tf_op jit(solution)/shard_map/while/body/eval_jaxpr/gkp,gpb->gkb/dot_general | solution.py:75
  144.1 2.1 %copy.61 = f32[128,5,512]{2,1,0:T(8,128)S(1)} copy(f32[128,5,512]{0,2,1:T(8,128)} %bitcast.135) | data formatting | bytes 2621440 | tf_op jit(solution)/shard_map/while/body/eval_jaxpr/reshape | solution.py:78
  146.3 5.8 %scatter_fusion = f32[64,5,512]{2,1,0:T(8,128)S(1)} fusion(f32[64,5,512]{2,1,0:T(8,128)S(1)} %get-tuple-element.193, s32[128]{0:T(128)S(1)} %fusion.58, f32[128,5,512]{2,1,0:T(8,128)S(1)} %copy.61), kind=kCustom, calls=%fused_computation.13.clone.clone.1 | custom fusion | flops 327680 | bytes 3932672 | tf_op jit(solution)/shard_map/while/body/eval_jaxpr/scatter-add | solution.py:79
  152.1 0.9 add_select_fusion.8
  153.9 1.0 dynamic-slice_bitcast_fusion.4
  154.9 0.9 dynamic-slice_bitcast_fusion.5
  156.0 2.8 %fusion.59 = f32[128,40,64]{2,1,0:T(8,128)} fusion(s32[128,128]{1,0:T(8,128)S(1)} %add_select_fusion.9, pred[128,8,128]{2,1,0:T(8,128)(4,1)S(1)} %iota_compare_fusion.8, bf16[128,5,128]{2,1,0:T(8,128)(2,1)S(1)} %pad_maximum_fusion.5), kind=kOutput, calls=%fused_computation.19.clone.1 | convolution fusion | flops 85590016 | bytes 1671168 | tf_op jit(solution)/shard_map/while/body/eval_jaxpr/gkp,gpb->gkb/dot_general | solution.py:75
  158.8 3.1 %copy.60 = f32[128,40,64]{0,2,1:T(8,128)} copy(f32[128,40,64]{2,1,0:T(8,128)} %fusion.59) | data formatting | bytes 2621440 | tf_op jit(solution)/shard_map/while/body/eval_jaxpr/gkp,gpb->gkb/dot_general | solution.py:75
  161.9 2.1 %copy.61 = f32[128,5,512]{2,1,0:T(8,128)S(1)} copy(f32[128,5,512]{0,2,1:T(8,128)} %bitcast.135) | data formatting | bytes 2621440 | tf_op jit(solution)/shard_map/while/body/eval_jaxpr/reshape | solution.py:78
  164.1 5.8 %scatter_fusion = f32[64,5,512]{2,1,0:T(8,128)S(1)} fusion(f32[64,5,512]{2,1,0:T(8,128)S(1)} %get-tuple-element.193, s32[128]{0:T(128)S(1)} %fusion.58, f32[128,5,512]{2,1,0:T(8,128)S(1)} %copy.61), kind=kCustom, calls=%fused_computation.13.clone.clone.1 | custom fusion | flops 327680 | bytes 3932672 | tf_op jit(solution)/shard_map/while/body/eval_jaxpr/scatter-add | solution.py:79
  169.9 0.9 add_select_fusion.8
  171.7 1.0 dynamic-slice_bitcast_fusion.4
  172.6 0.9 dynamic-slice_bitcast_fusion.5
  173.8 2.8 %fusion.59 = f32[128,40,64]{2,1,0:T(8,128)} fusion(s32[128,128]{1,0:T(8,128)S(1)} %add_select_fusion.9, pred[128,8,128]{2,1,0:T(8,128)(4,1)S(1)} %iota_compare_fusion.8, bf16[128,5,128]{2,1,0:T(8,128)(2,1)S(1)} %pad_maximum_fusion.5), kind=kOutput, calls=%fused_computation.19.clone.1 | convolution fusion | flops 85590016 | bytes 1671168 | tf_op jit(solution)/shard_map/while/body/eval_jaxpr/gkp,gpb->gkb/dot_general | solution.py:75
  176.5 3.1 %copy.60 = f32[128,40,64]{0,2,1:T(8,128)} copy(f32[128,40,64]{2,1,0:T(8,128)} %fusion.59) | data formatting | bytes 2621440 | tf_op jit(solution)/shard_map/while/body/eval_jaxpr/gkp,gpb->gkb/dot_general | solution.py:75
  179.7 2.1 %copy.61 = f32[128,5,512]{2,1,0:T(8,128)S(1)} copy(f32[128,5,512]{0,2,1:T(8,128)} %bitcast.135) | data formatting | bytes 2621440 | tf_op jit(solution)/shard_map/while/body/eval_jaxpr/reshape | solution.py:78
  181.8 5.8 %scatter_fusion = f32[64,5,512]{2,1,0:T(8,128)S(1)} fusion(f32[64,5,512]{2,1,0:T(8,128)S(1)} %get-tuple-element.193, s32[128]{0:T(128)S(1)} %fusion.58, f32[128,5,512]{2,1,0:T(8,128)S(1)} %copy.61), kind=kCustom, calls=%fused_computation.13.clone.clone.1 | custom fusion | flops 327680 | bytes 3932672 | tf_op jit(solution)/shard_map/while/body/eval_jaxpr/scatter-add | solution.py:79
  187.7 0.9 add_select_fusion.8
  189.5 1.0 dynamic-slice_bitcast_fusion.4
  190.4 0.9 dynamic-slice_bitcast_fusion.5
  191.5 2.8 %fusion.59 = f32[128,40,64]{2,1,0:T(8,128)} fusion(s32[128,128]{1,0:T(8,128)S(1)} %add_select_fusion.9, pred[128,8,128]{2,1,0:T(8,128)(4,1)S(1)} %iota_compare_fusion.8, bf16[128,5,128]{2,1,0:T(8,128)(2,1)S(1)} %pad_maximum_fusion.5), kind=kOutput, calls=%fused_computation.19.clone.1 | convolution fusion | flops 85590016 | bytes 1671168 | tf_op jit(solution)/shard_map/while/body/eval_jaxpr/gkp,gpb->gkb/dot_general | solution.py:75
  194.3 3.1 %copy.60 = f32[128,40,64]{0,2,1:T(8,128)} copy(f32[128,40,64]{2,1,0:T(8,128)} %fusion.59) | data formatting | bytes 2621440 | tf_op jit(solution)/shard_map/while/body/eval_jaxpr/gkp,gpb->gkb/dot_general | solution.py:75
  197.5 2.1 %copy.61 = f32[128,5,512]{2,1,0:T(8,128)S(1)} copy(f32[128,5,512]{0,2,1:T(8,128)} %bitcast.135) | data formatting | bytes 2621440 | tf_op jit(solution)/shard_map/while/body/eval_jaxpr/reshape | solution.py:78
  199.6 5.8 %scatter_fusion = f32[64,5,512]{2,1,0:T(8,128)S(1)} fusion(f32[64,5,512]{2,1,0:T(8,128)S(1)} %get-tuple-element.193, s32[128]{0:T(128)S(1)} %fusion.58, f32[128,5,512]{2,1,0:T(8,128)S(1)} %copy.61), kind=kCustom, calls=%fused_computation.13.clone.clone.1 | custom fusion | flops 327680 | bytes 3932672 | tf_op jit(solution)/shard_map/while/body/eval_jaxpr/scatter-add | solution.py:79
  205.9 0.9 fusion.21
  207.4 1.0 pad_maximum_fusion.3
  (89 shorter events, 10.8 us)
Async XLA Ops:
  0.6 38.9 %copy-start = (bf16[256,3,128]{2,0,1:T(8,128)(2,1)S(1)}, bf16[256,3,128]{2,0,1:T(8,128)(2,1)}, u32[]{:S(2)}) copy-start(bf16[256,3,128]{2,0,1:T(8,128)(2,1)} %param.16) | copy-start | bytes 589828
  0.6 5.2 %copy-start.1 = (s32[1,128]{1,0:T(1,128)S(1)}, s32[1,128]{1,0:T(1,128)}, u32[]{:S(2)}) copy-start(s32[1,128]{1,0:T(1,128)} %param.12) | copy-start | bytes 1540
  2.4 6.8 %copy-start.2 = (s32[256]{0:T(256)S(1)}, s32[256]{0:T(256)}, u32[]{:S(2)}) copy-start(s32[256]{0:T(256)} %param.11) | copy-start | bytes 3076
  5.8 6.9 %copy-start.3 = (s32[32768]{0:T(1024)S(1)}, s32[32768]{0:T(1024)}, u32[]{:S(2)}) copy-start(s32[32768]{0:T(1024)} %param.17) | copy-start | bytes 393220
  9.2 7.9 %copy-start.4 = (s32[256,128]{1,0:T(8,128)S(1)}, s32[256,128]{1,0:T(8,128)}, u32[]{:S(2)}) copy-start(s32[256,128]{1,0:T(8,128)} %param.13) | copy-start | bytes 393220
  17.1 19.3 %copy-start.5 = (bf16[256,128]{1,0:T(8,128)(2,1)S(1)}, bf16[256,128]{1,0:T(8,128)(2,1)}, u32[]{:S(2)}) copy-start(bf16[256,128]{1,0:T(8,128)(2,1)} %param.15) | copy-start | bytes 196612
  18.2 19.6 %copy-start.6 = (bf16[256,128]{1,0:T(8,128)(2,1)S(1)}, bf16[256,128]{1,0:T(8,128)(2,1)}, u32[]{:S(2)}) copy-start(bf16[256,128]{1,0:T(8,128)(2,1)} %param.14) | copy-start | bytes 196612
  19.1 35.8 %all-to-all-start = ((s32[128,4,129]{2,1,0:T(4,128)}), s32[128,4,129]{2,1,0:T(4,128)S(1)}, u32[]{:S(2)}, u32[]{:S(2)}) async-start(s32[128,4,129]{2,1,0:T(4,128)} %pad_add_fusion), calls=%async_computation | async-start | bytes 1048576 | tf_op jit(solution)/shard_map/all_to_all | solution.py:46
  54.9 36.9 %all-to-all-start.2 = ((bf16[512,5,128]{2,1,0:T(8,128)(2,1)}), bf16[512,5,128]{2,1,0:T(8,128)(2,1)S(1)}, u32[]{:S(2)}, u32[]{:S(2)}) async-start(bf16[512,5,128]{2,1,0:T(8,128)(2,1)} %copy.45), calls=%async_computation.2 | async-start | bytes 2097152 | tf_op jit(solution)/shard_map/all_to_all | solution.py:37
  101.6 21.4 %all-to-all-start.3 = ((bf16[512,5,128]{2,1,0:T(8,128)(2,1)}), bf16[512,5,128]{2,1,0:T(8,128)(2,1)S(1)}, u32[]{:S(2)}, u32[]{:S(2)}) async-start(bf16[512,5,128]{2,1,0:T(8,128)(2,1)} %pad_maximum_fusion.1), calls=%async_computation.3 | async-start | bytes 2097152 | tf_op jit(solution)/shard_map/all_to_all | solution.py:37
  105.9 13.6 %collective-permute-start = (s32[128]{0:T(128)S(1)}, s32[128]{0:T(128)S(1)}, u32[]{:S(2)}, u32[]{:S(2)}) collective-permute-start(s32[128]{0:T(128)S(1)} %get-tuple-element.143), channel_id=1, source_target_pairs={{0,1},{1,2},{2,3},{3,0},{4,5},{5,6},{6,7},{7,4},{8,9},{9,10},{10,1... | collective-permute-start | bytes 1544 | tf_op jit(solution)/shard_map/ppermute | solution.py:29
  109.8 12.6 %collective-permute-start.1 = (s32[128]{0:T(128)S(1)}, s32[128]{0:T(128)S(1)}, u32[]{:S(2)}, u32[]{:S(2)}) collective-permute-start(s32[128]{0:T(128)S(1)} %get-tuple-element.142), channel_id=1, source_target_pairs={{0,2},{1,3},{2,0},{3,1},{4,6},{5,7},{6,4},{7,5},{8,10},{9,11},{10,... | collective-permute-start | bytes 1544 | tf_op jit(solution)/shard_map/ppermute | solution.py:29
  114.4 8.0 %collective-permute-start.2 = (s32[128]{0:T(128)S(1)}, s32[128]{0:T(128)S(1)}, u32[]{:S(2)}, u32[]{:S(2)}) collective-permute-start(s32[128]{0:T(128)S(1)} %get-tuple-element.141), channel_id=1, source_target_pairs={{0,3},{1,0},{2,1},{3,2},{4,7},{5,4},{6,5},{7,6},{8,11},{9,8},{10,9... | collective-permute-start | bytes 1544 | tf_op jit(solution)/shard_map/ppermute | solution.py:29
  123.0 11.2 %all-to-all-start.1 = ((s32[4,128,128]{2,1,0:T(8,128)}), s32[4,128,128]{2,1,0:T(8,128)}, u32[]{:S(2)}, u32[]{:S(2)}) async-start(s32[4,128,128]{2,1,0:T(8,128)} %bitcast.23), calls=%async_computation.1 | async-start | bytes 524288 | tf_op jit(solution)/shard_map/all_to_all | solution.py:151
  134.3 71.6 %slice-start = ((f32[64,4,512]{2,1,0:T(4,128)}), f32[64,1,512]{2,1,0:T(1,128)S(1)}, s32[]{:S(2)}) async-start(f32[64,4,512]{2,1,0:T(4,128)} %param.18), calls=%async_computation.4 | async-start | bytes 262144 | tf_op jit(solution)/shard_map/slice | solution.py:158
  205.5 1.4 copy-start.7
  205.5 1.4 copy-start.8
  206.8 1.6 copy-start.9
